TPU v7x, 256 devices: a whole 4x4x8 slice. The times are simulated.
256 devices in a mesh: tile: 32 (over z_lo, y, core), lev: 8 (over x, z_hi).
Axes of the slice: x: 4, y: 4, z: 8 (z_hi: 2, z_lo: 4; z = z_hi * 4 + z_lo), core: 2. Of those that a mesh axis runs over, the one named last changes fastest.
Arguments:
- costate_ending_fields: float32 [4, 16, 32, 32, 128], P(None, 'lev', 'tile'), may hold values from -6 to 6
- costate_ending_elevation: float32 [32, 32, 128], P('tile'), may hold values from -6 to 6
- upstream_transport_coefficient: float32 [16, 32, 32, 128], P('lev', 'tile'), may hold values from 0.05 to 0.45
- eastward_spread_coefficient: float32 [32, 32, 128], P('tile'), may hold values from 0.02 to 0.2
- interface_blending_coefficient: float32 [16, 32, 32, 128], P('lev', 'tile'), may hold values from 0.02 to 0.3
- thickness_sensitivity: float32 [4, 16, 32, 32, 128], P(None, 'lev', 'tile'), may hold values from -1.75 to 1.75
- layer_velocity_factor: float32 [16, 32, 32, 128], P('lev', 'tile'), may hold values from 0.02 to 0.1
- western_join_turned: int32 [32], replicated, may hold values from 0 to 1
- predicted_thermal_skin: float32 [32, 32, 128], P('tile'), may hold values from -6 to 6
- predicted_elevation: float32 [32, 32, 128], P('tile'), may hold values from -6 to 6
- measured_quantity: float32 [8, 32, 32, 512], P('lev', 'tile'), may hold values from -6 to 6
- measurement_precision: float32 [8, 32, 32, 512], P('lev', 'tile'), may hold values from 0.05 to 0.3
- measurement_sort: int32 [8, 32, 32, 512], P('lev', 'tile'), may hold values from 0 to 1
- sampled_location: int32 [8, 32, 32, 512], P('lev', 'tile'), may hold values from 0 to 4095
- active_entry_numbers: int32 [8, 32, 32], P('lev', 'tile'), may hold values from 0 to 512, as said below
Outputs:
- adj_state_start: float32 [4, 16, 32, 32, 128], P(None, 'lev', 'tile')
- adj_height_start: float32 [32, 32, 128], P('tile')
Inputs may be any that keep to these rules, and one draw needn't show every extreme that they name: `western_join_turned`: 1 means a rotated seam. `active_entry_numbers`: slots at or above the count carry no record; in every draw some destination tile has all 512 slots live from every source tile in every level group.
All inputs are finite; a program needn't handle non-finite values.
Results may differ from a plain program's by a relative error of at most 0.0003.
Values sent between devices are 32-bit elements; how exact they have to be, the bound alone decides.
No kernel may reach another device: no remote copies, remote signals or barrier semaphores. Data moves between devices by JAX's collectives and lax.ppermute only.
A program may use at most 64 MiB of HBM per device.

v0:
```python
import jax
import jax.numpy as jnp
from jax import lax
from jax.sharding import PartitionSpec as P

OUT_SIGN = (1.0, 1.0, -1.0, 1.0)
SEAM_ORDER = (0, 1, 3, 2)


def shifted(value, axis, steps):
    count = lax.axis_size(axis)
    pairs = [(source, (source + steps) % count) for source in range(count)]
    return lax.ppermute(value, axis, pairs)


def from_behind(block, axis, distance):
    devices = range(lax.axis_size(axis))
    route = [(i - distance, i) for i in devices if i - distance in devices]
    return lax.ppermute(block, axis, route)


def adjoint_step(lam_state, lam_height, flow_l, diff_l, mix_l, stretch_l, weight_l, rotated):
    scaled = flow_l[None] * lam_state
    advect = jnp.concatenate([scaled[..., 1:], jnp.zeros_like(scaled[..., :1])], axis=-1) - scaled
    edge = scaled[..., 0]
    sign = jnp.array(OUT_SIGN, jnp.float32)[:, None, None]
    order = jnp.array(SEAM_ORDER, jnp.int32)
    outgoing = jnp.where(rotated, sign * edge[order][..., ::-1], edge)
    incoming = shifted(outgoing, "tile", -1)
    advect = advect.at[..., -1].add(incoming)
    next_row = jnp.concatenate(
        [lam_state[..., 1:, :], jnp.zeros_like(lam_state[..., :1, :])], axis=-2
    )
    face_y = diff_l[None, None] * (next_row - lam_state)
    mix_row = face_y - jnp.concatenate(
        [jnp.zeros_like(face_y[..., :1, :]), face_y[..., :-1, :]], axis=-2
    )
    below = from_behind(lam_state[:, :1], "lev", -1)
    lower = jnp.concatenate([lam_state[:, 1:], below], axis=1)
    face_z = mix_l[None] * (lower - lam_state)
    above = from_behind(face_z[:, -1:], "lev", 1)
    mix_col = face_z - jnp.concatenate([above, face_z[:, :-1]], axis=1)
    new_state = lam_state + advect + mix_row + mix_col
    new_state = new_state.at[2].add(weight_l * lam_height[None])
    column_part = jnp.sum(stretch_l * lam_state, axis=(0, 1))
    new_height = lam_height + lax.psum(column_part, "lev")
    return (new_state, new_height)


def per_device(
    costate_ending_fields,
    costate_ending_elevation,
    upstream_transport_coefficient,
    eastward_spread_coefficient,
    interface_blending_coefficient,
    thickness_sensitivity,
    layer_velocity_factor,
    western_join_turned,
    predicted_thermal_skin,
    predicted_elevation,
    measured_quantity,
    measurement_precision,
    measurement_sort,
    sampled_location,
    active_entry_numbers,
):
    lev_dev = costate_ending_fields.shape[1]
    rows = costate_ending_fields.shape[3]
    cols = costate_ending_fields.shape[4]
    slots = measured_quantity.shape[3]
    lev_index = lax.axis_index("lev")
    tile_index = lax.axis_index("tile")
    level_total = lev_dev * lax.axis_size("lev")
    global_level = lev_index * lev_dev + jnp.arange(lev_dev, dtype=jnp.int32)
    mix_l = (
        interface_blending_coefficient[:, 0]
        * (global_level < level_total - 1).astype(jnp.float32)[:, None, None]
    )
    row_mask = (jnp.arange(rows) < rows - 1).astype(jnp.float32)[:, None]
    diff_l = eastward_spread_coefficient[0] * row_mask
    flow_l = upstream_transport_coefficient[:, 0]
    stretch_l = thickness_sensitivity[:, :, 0]
    weight_l = layer_velocity_factor[:, 0]
    rotated = western_join_turned[tile_index] == 1
    live = jnp.arange(slots, dtype=jnp.int32)[None, :] < active_entry_numbers[0, 0][:, None]
    packet = jnp.stack(
        [
            measured_quantity[0, 0],
            jnp.where(live, measurement_precision[0, 0], 0.0),
            measurement_sort[0, 0].astype(jnp.float32),
            sampled_location[0, 0].astype(jnp.float32),
        ]
    )
    arrived = lax.all_to_all(packet, "tile", split_axis=1, concat_axis=1, tiled=True)
    record_kind = arrived[2].astype(jnp.int32)
    mesh_point = arrived[3].astype(jnp.int32)
    marine_dynamics = jnp.where(
        record_kind == 0,
        predicted_thermal_skin.reshape(-1)[mesh_point],
        predicted_elevation.reshape(-1)[mesh_point],
    )
    misfit = arrived[1] * (marine_dynamics - arrived[0])
    target = (record_kind * (rows * cols) + mesh_point).reshape(-1)
    maps = (
        jnp.zeros((2 * rows * cols,), jnp.float32)
        .at[target]
        .add(misfit.reshape(-1))
        .reshape(2, rows, cols)
    )
    maps = lax.psum(maps, "lev")
    lam_state = costate_ending_fields[:, :, 0]
    lam_state = lam_state.at[0, 0].add(jnp.where(lev_index == 0, maps[0], 0.0))
    lam_height = costate_ending_elevation[0] + maps[1]
    for turn in range(2):
        lam_state, lam_height = adjoint_step(
            lam_state, lam_height, flow_l, diff_l, mix_l, stretch_l, weight_l, rotated
        )
    return (lam_state[:, :, None], lam_height[None])


def solution(mesh):
    placed = (
        P(None, "lev", "tile", None, None),
        P("tile", None, None),
        P("lev", "tile", None, None),
        P("tile", None, None),
        P("lev", "tile", None, None),
        P(None, "lev", "tile", None, None),
        P("lev", "tile", None, None),
        P(),
        P("tile", None, None),
        P("tile", None, None),
        P("lev", "tile", None, None),
        P("lev", "tile", None, None),
        P("lev", "tile", None, None),
        P("lev", "tile", None, None),
        P("lev", "tile", None),
    )
    return jax.shard_map(
        per_device,
        mesh=mesh,
        in_specs=placed,
        out_specs=(P(None, "lev", "tile", None, None), P("tile", None, None)),
        check_vma=False,
    )
```

profile of v0, /device:TPU:38, one launch (start us, length us, event | category | flops | bytes accessed | tf_op | source)
XLA Modules:
  0.0 480.6 jit_solution(5255978705896090962)
XLA Ops:
  0.7 0.9 stack_squeeze.3
  3.5 1.0 pad_maximum_fusion
  4.5 8.9 %all-to-all-start = ((f32[4,32,512]{2,0,1:T(4,128)}), f32[4,32,512]{2,0,1:T(4,128)S(1)}, u32[]{:S(2)}, u32[]{:S(2)}) async-start(f32[4,32,512]{2,0,1:T(4,128)} %pad_maximum_fusion), calls=%async_computation | async-start | bytes 524288 | tf_op jit(solution)/shard_map/all_to_all | solution.py:94
  19.1 4.3 all-to-all-done
  23.9 90.5 %gather_fusion.1 = f32[16384]{0:T(1024)S(1)} fusion(f32[4096]{0:T(1024)S(1)} %bitcast.73, s32[16384]{0:T(1024)S(1)} %broadcast_clamp_fusion), kind=kCustom, calls=%fused_computation.1 | custom fusion | bytes 196608 | tf_op jit(solution)/shard_map/gather | solution.py:100
  114.5 90.5 %gather_fusion = f32[16384]{0:T(1024)S(1)} fusion(f32[4096]{0:T(1024)S(1)} %bitcast.74, s32[16384]{0:T(1024)S(1)} %broadcast_clamp_fusion), kind=kCustom, calls=%fused_computation | custom fusion | bytes 196608 | tf_op jit(solution)/shard_map/gather | solution.py:99
  205.4 85.8 %scatter_custom_fusion = f32[8192]{0:T(1024)S(1)} fusion(s32[16384]{0:T(1024)S(1)} %bitcast.86, f32[16384]{0:T(1024)S(1)} %subtract_multiply_fusion.2, f32[]{:T(128)} %constant.154.clone.1), kind=kCustom, calls=%fused_computation.50 | custom fusion | flops 16384 | bytes 32772 | tf_op jit(solution)/shard_map/scatter-add | solution.py:107
  291.4 54.0 %psum.21 = f32[2,32,128]{1,2,0:T(8,128)S(1)} all-reduce(f32[2,32,128]{1,2,0:T(8,128)S(1)} %copy.109), channel_id=1, replica_groups=mesh['tile'=32,'lev'=8] {'lev'}, use_global_device_ids=true, to_apply=%region_1.2 | all-reduce | flops 8192 | bytes 65536 | tf_op jit(solution)/shard_map/psum | solution.py:110
  345.4 1.6 scatter-add.25
  347.5 1.9 collective-permute-start.1
  350.0 12.1 %collective-permute-done.1 = f32[4,1,32,128]{2,1,0,3:T(1,128)S(1)} collective-permute-done((f32[4,1,32,128]{2,1,0,3:T(1,128)S(1)}, f32[4,1,32,128]{2,1,0,3:T(1,128)S(1)}, u32[]{:S(2)}, u32[]{:S(2)}) %collective-permute-start.1) | collective-permute-done | bytes 65568 | tf_op jit(solution)/shard_map/ppermute | solution.py:19
  362.1 1.2 broadcast_multiply_fusion.1
  365.6 1.9 collective-permute-start.2
  367.5 17.1 %collective-permute-done.2 = f32[4,1,32,128]{2,1,0,3:T(1,128)S(1)} collective-permute-done((f32[4,1,32,128]{2,1,0,3:T(1,128)S(1)}, f32[4,1,32,128]{2,1,0,3:T(1,128)S(1)}, u32[]{:S(2)}, u32[]{:S(2)}) %collective-permute-start.2) | collective-permute-done | bytes 65568 | tf_op jit(solution)/shard_map/ppermute | solution.py:19
  384.7 1.2 fusion.1
  386.0 1.1 fusion.17
  387.1 2.6 collective-permute-start.4
  390.7 16.0 %collective-permute-done.4 = f32[4,1,32,128]{2,1,0,3:T(1,128)S(1)} collective-permute-done((f32[4,1,32,128]{2,1,0,3:T(1,128)S(1)}, f32[4,1,32,128]{2,1,0,3:T(1,128)S(1)}, u32[]{:S(2)}, u32[]{:S(2)}) %collective-permute-start.4) | collective-permute-done | bytes 65568 | tf_op jit(solution)/shard_map/ppermute | solution.py:19
  407.4 3.7 fusion.5
  413.1 48.6 %all-reduce.6 = (f32[32,128]{0,1:T(8,128)S(1)}, f32[32,128]{0,1:T(8,128)S(1)}) all-reduce(f32[32,128]{0,1:T(8,128)S(1)} %copy-done.8, f32[32,128]{0,1:T(8,128)S(1)} %copy-done.7), channel_id=1, replica_groups=mesh['tile'=32,'lev'=8] {'lev'}, use_global_device_ids=true, to_apply=%region_3.4 | all-reduce | flops 8192 | bytes 65536 | tf_op jit(solution)/shard_map/psum | solution.py:46
  462.5 7.3 %collective-permute-start.5 = (f32[4,1,32,128]{2,1,0,3:T(1,128)S(1)}, f32[4,1,32,128]{2,1,0,3:T(1,128)S(1)}, u32[]{:S(2)}, u32[]{:S(2)}) collective-permute-start(f32[4,1,32,128]{2,1,0,3:T(1,128)S(1)} %get-tuple-element.81), channel_id=1, source_target_pairs={{0,1},{1,2},{2,3},{3,4},{4,5},{5,6},{6,7},{8,9},{9,10},{10,11},{11... | collective-permute-start | bytes 196616 | tf_op jit(solution)/shard_map/ppermute | solution.py:19
  469.9 8.4 %collective-permute-done.5 = f32[4,1,32,128]{2,1,0,3:T(1,128)S(1)} collective-permute-done((f32[4,1,32,128]{2,1,0,3:T(1,128)S(1)}, f32[4,1,32,128]{2,1,0,3:T(1,128)S(1)}, u32[]{:S(2)}, u32[]{:S(2)}) %collective-permute-start.5) | collective-permute-done | bytes 65568 | tf_op jit(solution)/shard_map/ppermute | solution.py:19
  478.2 1.2 fusion.3
  479.6 1.0 copy.118
  (106 shorter events, 15.7 us)
Async XLA Ops:
  0.6 23.3 %copy-start = (f32[1,32,128]{2,1,0:T(8,128)S(1)}, f32[1,32,128]{2,1,0:T(8,128)}, u32[]{:S(2)}) copy-start(f32[1,32,128]{2,1,0:T(8,128)} %param.38) | copy-start | bytes 49156
  0.6 0.9 copy-start.12
  1.6 0.8 copy-start.13
  2.4 0.8 copy-start.14
  2.4 0.8 copy-start.21
  4.5 9.0 %copy-start.19 = (f32[1,32,128]{2,1,0:T(8,128)S(1)}, f32[1,32,128]{2,1,0:T(8,128)}, u32[]{:S(2)}) copy-start(f32[1,32,128]{2,1,0:T(8,128)} %param.32) | copy-start | bytes 49156
  4.5 9.0 %copy-start.10 = (f32[4,2,1,32,128]{4,3,2,1,0:T(8,128)S(1)}, f32[4,2,1,32,128]{4,3,2,1,0:T(8,128)}, u32[]{:S(2)}) copy-start(f32[4,2,1,32,128]{4,3,2,1,0:T(8,128)} %param.29) | copy-start | bytes 393220
  4.5 19.0 %all-to-all-start = ((f32[4,32,512]{2,0,1:T(4,128)}), f32[4,32,512]{2,0,1:T(4,128)S(1)}, u32[]{:S(2)}, u32[]{:S(2)}) async-start(f32[4,32,512]{2,0,1:T(4,128)} %pad_maximum_fusion), calls=%async_computation | async-start | bytes 524288 | tf_op jit(solution)/shard_map/all_to_all | solution.py:94
  15.6 0.8 copy-start.15
  17.1 345.1 %copy-start.2 = (f32[2,32,128]{1,0,2:T(2,128)}, f32[2,32,128]{1,0,2:T(2,128)S(1)}, u32[]{:S(2)}) copy-start(f32[2,32,128]{1,0,2:T(2,128)S(1)} %copy.111) | copy-start | bytes 98308
  23.9 90.6 %copy-start.1 = (f32[1,32,128]{2,1,0:T(8,128)S(1)}, f32[1,32,128]{2,1,0:T(8,128)}, u32[]{:S(2)}) copy-start(f32[1,32,128]{2,1,0:T(8,128)} %param.37) | copy-start | bytes 49156
  347.5 14.7 %collective-permute-start.1 = (f32[4,1,32,128]{2,1,0,3:T(1,128)S(1)}, f32[4,1,32,128]{2,1,0,3:T(1,128)S(1)}, u32[]{:S(2)}, u32[]{:S(2)}) collective-permute-start(f32[4,1,32,128]{2,1,0,3:T(1,128)S(1)} %get-tuple-element.91), channel_id=1, source_target_pairs={{1,0},{2,1},{3,2},{4,3},{5,4},{6,5},{7,6},{9,8},{10,9},{11,10},{12... | collective-permute-start | bytes 196616 | tf_op jit(solution)/shard_map/ppermute | solution.py:19
  349.4 36.4 %copy-start.5 = (f32[32,128]{0,1:T(8,128)}, f32[32,128]{0,1:T(8,128)S(1)}, u32[]{:S(2)}) copy-start(f32[32,128]{0,1:T(8,128)S(1)} %fusion.9) | copy-start | bytes 49156
  364.8 2.7 collective-permute-start
  365.6 19.1 %collective-permute-start.2 = (f32[4,1,32,128]{2,1,0,3:T(1,128)S(1)}, f32[4,1,32,128]{2,1,0,3:T(1,128)S(1)}, u32[]{:S(2)}, u32[]{:S(2)}) collective-permute-start(f32[4,1,32,128]{2,1,0,3:T(1,128)S(1)} %get-tuple-element.88), channel_id=1, source_target_pairs={{0,1},{1,2},{2,3},{3,4},{4,5},{5,6},{6,7},{8,9},{9,10},{10,11},{11... | collective-permute-start | bytes 196616 | tf_op jit(solution)/shard_map/ppermute | solution.py:19
  386.0 3.7 copy-start.11
  387.1 19.6 %collective-permute-start.4 = (f32[4,1,32,128]{2,1,0,3:T(1,128)S(1)}, f32[4,1,32,128]{2,1,0,3:T(1,128)S(1)}, u32[]{:S(2)}, u32[]{:S(2)}) collective-permute-start(f32[4,1,32,128]{2,1,0,3:T(1,128)S(1)} %get-tuple-element.84), channel_id=1, source_target_pairs={{1,0},{2,1},{3,2},{4,3},{5,4},{6,5},{7,6},{9,8},{10,9},{11,10},{12... | collective-permute-start | bytes 196616 | tf_op jit(solution)/shard_map/ppermute | solution.py:19
  390.1 17.3 %copy-start.3 = (f32[2,32,128]{1,0,2:T(2,128)S(1)}, f32[2,32,128]{1,0,2:T(2,128)}, u32[]{:S(2)}) copy-start(f32[2,32,128]{1,0,2:T(2,128)} %copy-done.2) | copy-start | bytes 98308
  390.1 17.3 %copy-start.4 = (f32[4,1,32,128]{2,1,0,3:T(1,128)S(1)}, f32[4,1,32,128]{2,1,0,3:T(1,128)}, u32[]{:S(2)}) copy-start(f32[4,1,32,128]{2,1,0,3:T(1,128)} %get-tuple-element.83) | copy-start | bytes 196612
  411.9 58.0 %collective-permute-start.3 = (f32[4,2,32]{2,1,0:T(2,128)S(1)}, f32[4,2,32]{2,1,0:T(2,128)S(1)}, u32[]{:S(2)}, u32[]{:S(2)}) collective-permute-start(f32[4,2,32]{2,1,0:T(2,128)S(1)} %multiply_select_fusion), channel_id=1, source_target_pairs={{0,248},{8,0},{16,8},{24,16},{32,24},{40,32},{48,40},{56,48},{64,5... | collective-permute-start | bytes 3080 | tf_op jit(solution)/shard_map/ppermute | solution.py:13
  412.3 0.8 copy-start.7
  412.3 0.9 copy-start.8
  413.1 48.7 %copy-start.6 = (f32[32,128]{0,1:T(8,128)S(1)}, f32[32,128]{0,1:T(8,128)}, u32[]{:S(2)}) copy-start(f32[32,128]{0,1:T(8,128)} %copy-done.5) | copy-start | bytes 49156
  462.5 15.7 %collective-permute-start.5 = (f32[4,1,32,128]{2,1,0,3:T(1,128)S(1)}, f32[4,1,32,128]{2,1,0,3:T(1,128)S(1)}, u32[]{:S(2)}, u32[]{:S(2)}) collective-permute-start(f32[4,1,32,128]{2,1,0,3:T(1,128)S(1)} %get-tuple-element.81), channel_id=1, source_target_pairs={{0,1},{1,2},{2,3},{3,4},{4,5},{5,6},{6,7},{8,9},{9,10},{10,11},{11... | collective-permute-start | bytes 196616 | tf_op jit(solution)/shard_map/ppermute | solution.py:19
  (7 other events, 4.9 us)
where the time goes:
time: 481 us
  local copies, waits for them, and re-layouts  199 us (41%)
  blocking collectives  103 us (21%)
  other arithmetic  96.2 us (20%)
  waiting for transfers between devices  57.9 us (12%)
  starting transfers between devices  22.7 us (5%)
    gather x1, local copies, waits for them, and re-layouts, per_device(): predicted_elevation.reshape(-1)[mesh_point]  90.5 us
    gather x1, local copies, waits for them, and re-layouts, per_device(): predicted_thermal_skin.reshape(-1)[mesh_point]  90.5 us
    scatter-add x1, other arithmetic, per_device(): maps = jnp.zeros((2 * rows * cols,), jnp.float32).at[target].add(misfit.r...  85.8 us
    psum x1, blocking collectives, per_device(): maps = lax.psum(maps, 'lev')  54 us
    ppermute x4, waiting for transfers between devices, from_behind(): return lax.ppermute(block, axis, route)  53.6 us
    psum x1, blocking collectives, adjoint_step(): new_height = lam_height + lax.psum(column_part, 'lev')  48.6 us
    ppermute x4, starting transfers between devices, from_behind(): return lax.ppermute(block, axis, route)  13.7 us
  transfers between devices with their start and end apart: 7, of which 5 were waited for; matrix products, arithmetic and copies ran while one was open for 1% of the time, Pallas kernels for 0%

commit v1 on v0

--- a/solution.py
+++ b/solution.py
@@ -43,7 +43,7 @@
     new_state = lam_state + advect + mix_row + mix_col
     new_state = new_state.at[2].add(weight_l * lam_height[None])
     column_part = jnp.sum(stretch_l * lam_state, axis=(0, 1))
-    new_height = lam_height + lax.psum(column_part, "lev")
+    new_height = lam_height + jnp.sum(lax.all_gather(column_part, "lev"), axis=0)
     return (new_state, new_height)
 
 

time: 481 us -> 519 us (1.079)
  blocking collectives: 103 us -> 137 us
    all_gather x0 -> x2, blocking collectives: none -> 87.2 us  [adjoint_step(): lax.all_gather(column_part, 'lev')]
    psum x1 -> x0, blocking collectives: 48.6 us -> none  [adjoint_step(): new_height = lam_height + lax.psum(column_part, 'lev')]
where the time goes in v1:
time: 519 us; the launch traced here: 517 us
  local copies, waits for them, and re-layouts  200 us (39%)
  blocking collectives  137 us (26%)
  other arithmetic  98.3 us (19%)
  waiting for transfers between devices  58.8 us (11%)
  starting transfers between devices  21.4 us (4%)
    gather x1, local copies, waits for them, and re-layouts, per_device(): predicted_elevation.reshape(-1)[mesh_point]  90.5 us
    gather x1, local copies, waits for them, and re-layouts, per_device(): predicted_thermal_skin.reshape(-1)[mesh_point]  90.5 us
    all_gather x2, blocking collectives, adjoint_step(): lax.all_gather(column_part, 'lev')  87.2 us
    scatter-add x1, other arithmetic, per_device(): maps = jnp.zeros((2 * rows * cols,), jnp.float32).at[target].add(misfit.r...  85.8 us
    ppermute x4, waiting for transfers between devices, from_behind(): return lax.ppermute(block, axis, route)  54.3 us
    psum x1, blocking collectives, per_device(): maps = lax.psum(maps, 'lev')  49.7 us
    ppermute x4, starting transfers between devices, from_behind(): return lax.ppermute(block, axis, route)  12.5 us
  transfers between devices with their start and end apart: 7, of which 5 were waited for; matrix products, arithmetic and copies ran while one was open for 1% of the time, Pallas kernels for 0%

profile of v1, /device:TPU:38, one launch (start us, length us, event | category | flops | bytes accessed | tf_op | source)
XLA Modules:
  0.0 517.0 jit_solution(357013659498480095)
XLA Ops:
  3.5 1.0 pad_maximum_fusion
  4.5 8.9 %all-to-all-start = ((f32[4,32,512]{2,0,1:T(4,128)}), f32[4,32,512]{2,0,1:T(4,128)S(1)}, u32[]{:S(2)}, u32[]{:S(2)}) async-start(f32[4,32,512]{2,0,1:T(4,128)} %pad_maximum_fusion), calls=%async_computation | async-start | bytes 524288 | tf_op jit(solution)/shard_map/all_to_all | solution.py:94
  18.9 4.5 all-to-all-done
  23.9 90.5 %gather_fusion.1 = f32[16384]{0:T(1024)S(1)} fusion(f32[4096]{0:T(1024)S(1)} %bitcast.82, s32[16384]{0:T(1024)S(1)} %broadcast_clamp_fusion), kind=kCustom, calls=%fused_computation.1 | custom fusion | bytes 196608 | tf_op jit(solution)/shard_map/gather | solution.py:100
  114.5 90.5 %gather_fusion = f32[16384]{0:T(1024)S(1)} fusion(f32[4096]{0:T(1024)S(1)} %bitcast.83, s32[16384]{0:T(1024)S(1)} %broadcast_clamp_fusion), kind=kCustom, calls=%fused_computation | custom fusion | bytes 196608 | tf_op jit(solution)/shard_map/gather | solution.py:99
  205.4 85.8 %scatter_custom_fusion = f32[8192]{0:T(1024)S(1)} fusion(s32[16384]{0:T(1024)S(1)} %bitcast.96, f32[16384]{0:T(1024)S(1)} %subtract_multiply_fusion.2, f32[]{:T(128)} %constant.154.clone.1), kind=kCustom, calls=%fused_computation.50 | custom fusion | flops 16384 | bytes 32772 | tf_op jit(solution)/shard_map/scatter-add | solution.py:107
  291.2 49.7 %psum.7 = f32[2,32,128]{2,1,0:T(8,128)S(1)} all-reduce(f32[2,32,128]{2,1,0:T(8,128)S(1)} %bitcast.94), channel_id=1, replica_groups=mesh['tile'=32,'lev'=8] {'lev'}, use_global_device_ids=true, to_apply=%region_1.2 | all-reduce | flops 8192 | bytes 65536 | tf_op jit(solution)/shard_map/psum | solution.py:110
  341.1 1.6 scatter-add.25
  343.1 1.9 collective-permute-start.1
  345.8 12.0 %collective-permute-done.1 = f32[4,1,32,128]{2,1,0,3:T(1,128)S(1)} collective-permute-done((f32[4,1,32,128]{2,1,0,3:T(1,128)S(1)}, f32[4,1,32,128]{2,1,0,3:T(1,128)S(1)}, u32[]{:S(2)}, u32[]{:S(2)}) %collective-permute-start.1) | collective-permute-done | bytes 65568 | tf_op jit(solution)/shard_map/ppermute | solution.py:19
  358.5 2.2 broadcast_multiply_fusion.1
  363.0 1.9 collective-permute-start.2
  365.0 18.1 %collective-permute-done.2 = f32[4,1,32,128]{2,1,0,3:T(1,128)S(1)} collective-permute-done((f32[4,1,32,128]{2,1,0,3:T(1,128)S(1)}, f32[4,1,32,128]{2,1,0,3:T(1,128)S(1)}, u32[]{:S(2)}, u32[]{:S(2)}) %collective-permute-start.2) | collective-permute-done | bytes 65568 | tf_op jit(solution)/shard_map/ppermute | solution.py:19
  383.0 1.2 fusion.1
  384.4 1.1 fusion.18
  385.5 2.9 collective-permute-start.4
  389.4 15.3 %collective-permute-done.4 = f32[4,1,32,128]{2,1,0,3:T(1,128)S(1)} collective-permute-done((f32[4,1,32,128]{2,1,0,3:T(1,128)S(1)}, f32[4,1,32,128]{2,1,0,3:T(1,128)S(1)}, u32[]{:S(2)}, u32[]{:S(2)}) %collective-permute-start.4) | collective-permute-done | bytes 65568 | tf_op jit(solution)/shard_map/ppermute | solution.py:19
  405.4 3.7 fusion.5
  411.0 43.0 %all-gather = f32[256,128]{1,0:T(8,128)S(1)} all-gather(f32[32,128]{1,0:T(8,128)S(1)} %copy.140), channel_id=2, replica_groups=mesh['tile'=32,'lev'=8] {'lev'}, dimensions={0}, use_global_device_ids=true | all-gather | bytes 147456 | tf_op jit(solution)/shard_map/all_gather | solution.py:46
  454.0 44.2 %all-gather.1 = f32[256,128]{1,0:T(8,128)S(1)} all-gather(f32[32,128]{1,0:T(8,128)S(1)} %copy.143), channel_id=3, replica_groups=mesh['tile'=32,'lev'=8] {'lev'}, dimensions={0}, use_global_device_ids=true | all-gather | bytes 147456 | tf_op jit(solution)/shard_map/all_gather | solution.py:46
  500.0 5.7 %collective-permute-start.5 = (f32[4,1,32,128]{2,1,0,3:T(1,128)S(1)}, f32[4,1,32,128]{2,1,0,3:T(1,128)S(1)}, u32[]{:S(2)}, u32[]{:S(2)}) collective-permute-start(f32[4,1,32,128]{2,1,0,3:T(1,128)S(1)} %get-tuple-element.79), channel_id=1, source_target_pairs={{0,1},{1,2},{2,3},{3,4},{4,5},{5,6},{6,7},{8,9},{9,10},{10,11},{11... | collective-permute-start | bytes 196616 | tf_op jit(solution)/shard_map/ppermute | solution.py:19
  505.8 9.0 %collective-permute-done.5 = f32[4,1,32,128]{2,1,0,3:T(1,128)S(1)} collective-permute-done((f32[4,1,32,128]{2,1,0,3:T(1,128)S(1)}, f32[4,1,32,128]{2,1,0,3:T(1,128)S(1)}, u32[]{:S(2)}, u32[]{:S(2)}) %collective-permute-start.5) | collective-permute-done | bytes 65568 | tf_op jit(solution)/shard_map/ppermute | solution.py:19
  514.7 1.1 fusion.3
  516.1 1.0 copy.144
  (113 shorter events, 18.3 us)
Async XLA Ops:
  0.6 23.3 %copy-start = (f32[1,32,128]{2,1,0:T(8,128)S(1)}, f32[1,32,128]{2,1,0:T(8,128)}, u32[]{:S(2)}) copy-start(f32[1,32,128]{2,1,0:T(8,128)} %param.38) | copy-start | bytes 49156
  0.6 0.9 copy-start.13
  1.6 0.8 copy-start.14
  2.4 0.8 copy-start.15
  2.4 0.8 copy-start.23
  4.5 8.9 %copy-start.21 = (f32[1,32,128]{2,1,0:T(8,128)S(1)}, f32[1,32,128]{2,1,0:T(8,128)}, u32[]{:S(2)}) copy-start(f32[1,32,128]{2,1,0:T(8,128)} %param.32) | copy-start | bytes 49156
  4.5 19.0 %all-to-all-start = ((f32[4,32,512]{2,0,1:T(4,128)}), f32[4,32,512]{2,0,1:T(4,128)S(1)}, u32[]{:S(2)}, u32[]{:S(2)}) async-start(f32[4,32,512]{2,0,1:T(4,128)} %pad_maximum_fusion), calls=%async_computation | async-start | bytes 524288 | tf_op jit(solution)/shard_map/all_to_all | solution.py:94
  13.5 0.8 copy-start.20
  15.1 0.9 copy-start.11
  15.9 342.6 %copy-start.2 = (f32[2,32,128]{1,0,2:T(2,128)}, f32[2,32,128]{1,0,2:T(2,128)S(1)}, u32[]{:S(2)}) copy-start(f32[2,32,128]{1,0,2:T(2,128)S(1)} %copy.134) | copy-start | bytes 98308
  23.9 90.6 %copy-start.1 = (f32[1,32,128]{2,1,0:T(8,128)S(1)}, f32[1,32,128]{2,1,0:T(8,128)}, u32[]{:S(2)}) copy-start(f32[1,32,128]{2,1,0:T(8,128)} %param.37) | copy-start | bytes 49156
  341.0 4.1 copy-start.9
  342.7 2.4 copy-start.16
  343.1 14.6 %collective-permute-start.1 = (f32[4,1,32,128]{2,1,0,3:T(1,128)S(1)}, f32[4,1,32,128]{2,1,0,3:T(1,128)S(1)}, u32[]{:S(2)}, u32[]{:S(2)}) collective-permute-start(f32[4,1,32,128]{2,1,0,3:T(1,128)S(1)} %get-tuple-element.89), channel_id=1, source_target_pairs={{1,0},{2,1},{3,2},{4,3},{5,4},{6,5},{7,6},{9,8},{10,9},{11,10},{12... | collective-permute-start | bytes 196616 | tf_op jit(solution)/shard_map/ppermute | solution.py:19
  362.3 2.7 collective-permute-start
  363.0 20.0 %collective-permute-start.2 = (f32[4,1,32,128]{2,1,0,3:T(1,128)S(1)}, f32[4,1,32,128]{2,1,0,3:T(1,128)S(1)}, u32[]{:S(2)}, u32[]{:S(2)}) collective-permute-start(f32[4,1,32,128]{2,1,0,3:T(1,128)S(1)} %get-tuple-element.86), channel_id=1, source_target_pairs={{0,1},{1,2},{2,3},{3,4},{4,5},{5,6},{6,7},{8,9},{9,10},{10,11},{11... | collective-permute-start | bytes 196616 | tf_op jit(solution)/shard_map/ppermute | solution.py:19
  384.4 4.1 copy-start.12
  385.5 19.2 %collective-permute-start.4 = (f32[4,1,32,128]{2,1,0,3:T(1,128)S(1)}, f32[4,1,32,128]{2,1,0,3:T(1,128)S(1)}, u32[]{:S(2)}, u32[]{:S(2)}) collective-permute-start(f32[4,1,32,128]{2,1,0,3:T(1,128)S(1)} %get-tuple-element.82), channel_id=1, source_target_pairs={{1,0},{2,1},{3,2},{4,3},{5,4},{6,5},{7,6},{9,8},{10,9},{11,10},{12... | collective-permute-start | bytes 196616 | tf_op jit(solution)/shard_map/ppermute | solution.py:19
  388.8 16.6 %copy-start.3 = (f32[2,32,128]{1,0,2:T(2,128)S(1)}, f32[2,32,128]{1,0,2:T(2,128)}, u32[]{:S(2)}) copy-start(f32[2,32,128]{1,0,2:T(2,128)} %copy-done.2) | copy-start | bytes 98308
  388.8 16.6 %copy-start.4 = (f32[4,1,32,128]{2,1,0,3:T(1,128)S(1)}, f32[4,1,32,128]{2,1,0,3:T(1,128)}, u32[]{:S(2)}) copy-start(f32[4,1,32,128]{2,1,0,3:T(1,128)} %get-tuple-element.81) | copy-start | bytes 196612
  409.1 0.8 copy-start.6
  409.2 1.8 copy-start.5
  410.9 94.9 %collective-permute-start.3 = (f32[4,2,32]{2,1,0:T(2,128)S(1)}, f32[4,2,32]{2,1,0:T(2,128)S(1)}, u32[]{:S(2)}, u32[]{:S(2)}) collective-permute-start(f32[4,2,32]{2,1,0:T(2,128)S(1)} %multiply_select_fusion), channel_id=1, source_target_pairs={{0,248},{8,0},{16,8},{24,16},{32,24},{40,32},{48,40},{56,48},{64,5... | collective-permute-start | bytes 3080 | tf_op jit(solution)/shard_map/ppermute | solution.py:13
  500.0 14.7 %collective-permute-start.5 = (f32[4,1,32,128]{2,1,0,3:T(1,128)S(1)}, f32[4,1,32,128]{2,1,0,3:T(1,128)S(1)}, u32[]{:S(2)}, u32[]{:S(2)}) collective-permute-start(f32[4,1,32,128]{2,1,0,3:T(1,128)S(1)} %get-tuple-element.79), channel_id=1, source_target_pairs={{0,1},{1,2},{2,3},{3,4},{4,5},{5,6},{6,7},{8,9},{9,10},{10,11},{11... | collective-permute-start | bytes 196616 | tf_op jit(solution)/shard_map/ppermute | solution.py:19
  (9 other events, 6.4 us)
